TPU v7x, 32 devices: a whole 2x2x4 slice. The times are simulated.
32 devices in a mesh: lat: 4 (over z), lon: 8 (over y, x, core).
Axes of the slice: x: 2, y: 2, z: 4, core: 2. Of those that a mesh axis runs over, the one named last changes fastest.
Arguments:
- state: bfloat16 [192, 64, 1024], P(None, 'lat', 'lon'), may hold values from -6 to 6
- depth_kernel: bfloat16 [192, 7, 7], replicated, may hold values from -0.875 to 0.875
- point_weight: bfloat16 [192, 192], replicated, may hold values from -0.4375 to 0.4375
- column_index: int32 [16384, 4], P(('lat', 'lon')), may hold values from 0 to 2047, as said below
- column_weight: bfloat16 [16384, 4], P(('lat', 'lon')), may hold values from 0.049804688 to 0.59765625
- owner: int32 [16384, 1], P(('lat', 'lon')), may hold values from 0 to 7; in each aligned block of 512 rows (0 to 511, 512 to 1023, ...) at most 64 rows name the same one
- observed: bfloat16 [16384, 137], P(('lat', 'lon')), may hold values from -6 to 6
- hidden_weight: bfloat16 [8, 192, 512], P('lon'), may hold values from -0.4375 to 0.4375
- level_weight: bfloat16 [8, 512, 137], P('lon'), may hold values from -0.25 to 0.25
- inverse_error: bfloat16 [8, 137], P('lon'), may hold values from 0.25 to 4
Outputs:
- gradient: bfloat16 [192, 64, 1024], P(None, 'lat', 'lon')
- departures: bfloat16 [16384, 137], P(('lat', 'lon'))
Inputs may be any that keep to these rules, and one draw needn't show every extreme that they name: `column_index`: the four columns of one grid box of the sounding's own tile: b, b + 1, b + 128, b + 129. `owner`: among the 512 soundings of one tile no instrument appears more than 64 times.
All inputs are finite; a program needn't handle non-finite values.
Results may differ from a plain program's by a relative error of at most 0.0085.
Values may be sent and summed in bfloat16 or wider, within the bound.
A program may use at most 128 MiB of HBM per device.

v0:
```python
import jax
import jax.numpy as jnp
from jax import lax
from jax.experimental import pallas as pl
from jax.experimental.pallas import tpu as pltpu
from jax.sharding import PartitionSpec as P

CAP = 64
F32 = jnp.float32
BF = jnp.bfloat16
VM = pl.BlockSpec(memory_space=pltpu.VMEM)


def nn(a, b):
    return jnp.dot(a, b, preferred_element_type=F32)


def nt(a, b):
    return lax.dot_general(a, b, (((1,), (1,)), ((), ())), preferred_element_type=F32)


def conv_group(x_ref, h_ref, k_ref, base, flip):
    rows = x_ref.shape[0]
    breadth = x_ref.shape[2]
    height = rows - 6
    lane = lax.broadcasted_iota(jnp.int32, (16, breadth), 1)
    taps = k_ref[pl.ds(base, 16), :]
    acc = [None] * height
    for col in range(7):
        shift = col - 3
        weights = []
        for row in range(7):
            t = (6 - row) * 8 + 6 - col if flip else row * 8 + col
            weights.append(jnp.broadcast_to(taps[:, t : t + 1], (16, breadth)))
        for r in range(rows):
            v = x_ref[r, pl.ds(base, 16), :].astype(F32)
            if shift:
                edge = h_ref[r, pl.ds(base, 16), :].astype(F32)
                mask = lane < shift if shift > 0 else lane >= breadth + shift
                v = pltpu.roll(jnp.where(mask, edge, v), (-shift) % breadth, 1)
            for row in range(7):
                i = r - row
                if 0 <= i < height:
                    term = weights[row] * v
                    acc[i] = term if acc[i] is None else acc[i] + term
    return acc


def prepare(owner, index, weight, obs_t, meta, wt_ref, p_ref, pt_ref, obs_slot):
    height, obs, breadth = wt_ref.shape
    slots = p_ref.shape[0]
    n = slots // CAP
    si = lax.broadcasted_iota(jnp.int32, (obs, obs), 0)
    sj = lax.broadcasted_iota(jnp.int32, (obs, obs), 1)
    earlier = jnp.where(si < sj, 1.0, 0.0).astype(BF)
    own = owner[...]
    hot = jnp.where(lax.broadcasted_iota(jnp.int32, (n, obs), 0) == own, 1.0, 0.0)
    within = jnp.sum(nn(hot.astype(BF), earlier) * hot, axis=0, keepdims=True)
    slot_row = own * CAP + within.astype(jnp.int32)
    corner = index[0:1, :].astype(F32)
    row0 = jnp.floor((corner + 0.5) / breadth)
    meta[...] = jnp.zeros_like(meta)
    meta[0:4, :] = weight[...].astype(F32)
    meta[4:5, :] = row0
    meta[5:6, :] = corner - row0 * breadth
    meta[6:7, :] = slot_row.astype(F32)
    by_obs = meta[...].T
    w = by_obs[:, 0:4]
    whole = by_obs.astype(jnp.int32)
    lane = lax.broadcasted_iota(jnp.int32, (obs, breadth), 1)
    r0 = jnp.broadcast_to(whole[:, 4:5], (obs, breadth))
    c0 = jnp.broadcast_to(whole[:, 5:6], (obs, breadth))
    zero = jnp.zeros((obs, breadth), F32)
    first = lane == c0
    second = lane == c0 + 1
    top = jnp.where(first, w[:, 0:1], jnp.where(second, w[:, 1:2], zero))
    bottom = jnp.where(first, w[:, 2:3], jnp.where(second, w[:, 3:4], zero))
    for r in range(height):
        wt_ref[r] = jnp.where(r0 == r, top, jnp.where(r0 == r - 1, bottom, zero)).astype(BF)
    place = lax.broadcasted_iota(jnp.int32, (slots, obs), 0) == slot_row
    p = jnp.where(place, 1.0, 0.0).astype(BF)
    p_ref[...] = p
    place = lax.broadcasted_iota(jnp.int32, (obs, slots), 1) == whole[:, 6:7]
    pt_ref[...] = jnp.where(place, 1.0, 0.0).astype(BF)
    obs_slot[...] = nt(p, obs_t[...]).astype(BF)


def remote(src, dst, send, recv, device):
    return pltpu.make_async_remote_copy(
        src_ref=src,
        dst_ref=dst,
        send_sem=send,
        recv_sem=recv,
        device_id=device,
        device_id_type=pl.DeviceIdType.MESH,
    )


def selector(breadth):
    s = lax.broadcasted_iota(jnp.int32, (8, breadth), 0)
    lane = lax.broadcasted_iota(jnp.int32, (8, breadth), 1)
    near = (s < 3) & (lane == s)
    far = (s > 4) & (lane == s + (breadth - 8))
    return jnp.where(near | far, 1.0, 0.0).astype(BF)


def copies(src, off, x, edge, right_in, left_in, send, recv, lats, lons):
    height = edge.shape[0]
    lat, lon = lax.axis_index("lat"), lax.axis_index("lon")
    left, right = lax.rem(lon + lons - 1, lons), lax.rem(lon + 1, lons)
    low, high, mid = pl.ds(0, 3), pl.ds(height + 3, 3), pl.ds(3, height)
    end = pl.ds(height - 3, 3)

    def make(i, a, b, device):
        return remote(a, b, send.at[i], recv.at[i], device)

    side = [
        make(2, edge, right_in.at[mid], {"lat": lat, "lon": left}),
        make(3, edge, left_in.at[mid], {"lat": lat, "lon": right}),
    ]
    u, d = lax.max(lat - 1, 0), lax.min(lat + 1, lats - 1)
    up = [
        make(0, src.at[pl.ds(off, 3)], x.at[high], {"lat": u, "lon": lon}),
        make(4, edge.at[low], right_in.at[high], {"lat": u, "lon": left}),
        make(5, edge.at[low], left_in.at[high], {"lat": u, "lon": right}),
    ]
    down = [
        make(1, src.at[pl.ds(off + height - 3, 3)], x.at[low], {"lat": d, "lon": lon}),
        make(6, edge.at[end], right_in.at[low], {"lat": d, "lon": left}),
        make(7, edge.at[end], left_in.at[low], {"lat": d, "lon": right}),
    ]
    return lat > 0, lat < lats - 1, up, down, side


def make_edges(src, edge):
    pick = selector(src.shape[2])

    def row(r, carry):
        edge[r] = nt(pick, src[3 + r]).astype(BF)
        return carry

    lax.fori_loop(0, edge.shape[0], row, 0, unroll=4)


def start_exchange(x, edge, right_in, left_in, send, recv, lats, lons):
    height = edge.shape[0]
    has_up, has_down, up, down, side = copies(
        x, 3, x, edge, right_in, left_in, send, recv, lats, lons
    )

    @pl.when(has_up)
    def _():
        for copy in up:
            copy.start()

    @pl.when(has_down)
    def _():
        for copy in down:
            copy.start()

    for copy in side:
        copy.start()
    for has, at in ((has_up, 0), (has_down, height + 3)):

        @pl.when(jnp.logical_not(has))
        def _():
            for ref in (x, right_in, left_in):
                ref[at : at + 3] = jnp.zeros((3,) + ref.shape[1:], BF)


def end_exchange(x, edge, right_in, left_in, halo, send, recv, lats, lons):
    has_up, has_down, up, down, side = copies(
        x, 3, x, edge, right_in, left_in, send, recv, lats, lons
    )

    @pl.when(has_up)
    def _():
        for copy in down:
            copy.wait_recv()
        for copy in up:
            copy.wait_send()

    @pl.when(has_down)
    def _():
        for copy in up:
            copy.wait_recv()
        for copy in down:
            copy.wait_send()

    for copy in side:
        copy.wait()
    pick = selector(x.shape[2])
    near = lax.broadcasted_iota(jnp.int32, (8, x.shape[1]), 0) < 4

    def row(r, carry):
        both = jnp.where(near, right_in[r].astype(F32), left_in[r].astype(F32))
        halo[r] = nn(both.T.astype(BF), pick).astype(BF)
        return carry

    lax.fori_loop(0, x.shape[0], row, 0, unroll=2)


def kernel(
    lats,
    lons,
    state,
    hw_ref,
    lw_ref,
    err_ref,
    owner,
    index,
    weight,
    obs_t,
    k_ref,
    pw_ref,
    out_ref,
    dep_ref,
    x1,
    x2,
    stage,
    meta,
    tap_rows,
    taps,
    pwt,
    halo,
    edge,
    right_in,
    left_in,
    ops,
    wt,
    p_mat,
    pt_mat,
    obs_slot,
    mixed,
    grid_f,
    total,
    prof,
    adj,
    mis,
    send,
    recv,
    op_send,
    op_recv,
):
    channels, height, breadth = state.shape
    levels = obs_t.shape[0]
    err_row = ops.shape[1] - 16
    lat, lon = lax.axis_index("lat"), lax.axis_index("lon")
    partner = lon + 1 - 2 * lax.rem(lon, 2)
    other = lax.rem(lon + lons - 1 + 2 * lax.rem(lon, 2), lons)
    half = lons // 2
    peers = [lax.rem(lon + 2 * j, lons) for j in range(1, half)]
    barrier = pltpu.get_barrier_semaphore()

    def greet(a, b):
        pl.semaphore_signal(
            barrier,
            inc=1,
            device_id={"lat": a, "lon": b},
            device_id_type=pl.DeviceIdType.MESH,
        )

    for b in [partner, other] + peers:
        greet(lat, b)

    @pl.when(lat > 0)
    def _():
        for b in (partner, lon, other):
            greet(lat - 1, b)

    @pl.when(lat < lats - 1)
    def _():
        for b in (partner, lon, other):
            greet(lat + 1, b)

    def turn(g, carry):
        at = pl.ds(pl.multiple_of(g * 16, 16), 16)
        stage[...] = state[at].astype(F32)
        for r in range(height):
            x1[3 + r, at, :] = stage[:, r, :].astype(BF)
        return carry

    lax.fori_loop(0, channels // 16, turn, 0)

    def wires(k):
        return edge.at[k], right_in.at[k], left_in.at[k]

    make_edges(x1, edge.at[0])
    ops[lon] = jnp.zeros(ops.shape[1:], BF)
    ops[lon, :channels, :] = hw_ref[0]
    ops[lon, channels : channels + levels, :] = lw_ref[0]
    ops[lon, err_row : err_row + 1, :levels] = err_ref[...]
    sides = lax.min(lat, 1) + lax.min(lats - 1 - lat, 1)
    pl.semaphore_wait(barrier, half + 1 + 3 * sides)
    start_exchange(x1, *wires(0), send.at[0], recv.at[0], lats, lons)
    mine = ops.at[lon]
    sends = [
        remote(mine, mine, op_send.at[j], op_recv.at[lon], {"lat": lat, "lon": b})
        for j, b in enumerate([partner] + peers)
    ]
    for copy in sends:
        copy.start()
    tap_rows[...] = jnp.zeros_like(tap_rows)
    for row in range(7):
        tap_rows[8 * row : 8 * row + 7, :] = k_ref[row].astype(F32)
    taps[...] = tap_rows[...].T
    pwt[...] = pw_ref[...].astype(F32).T.astype(BF)
    prepare(owner, index, weight, obs_t, meta, wt, p_mat, pt_mat, obs_slot)
    end_exchange(x1, *wires(0), halo, send.at[0], recv.at[0], lats, lons)

    def group(g, carry):
        base = pl.multiple_of(g * 16, 16)
        for i, v in enumerate(conv_group(x1, halo, taps, base, False)):
            mixed[i, pl.ds(base, 16), :] = v.astype(BF)
        return carry

    lax.fori_loop(0, channels // 16, group, 0)

    forwards = []
    for j, b in enumerate(peers):
        copy = remote(
            ops.at[b], ops.at[b], op_send.at[half + j], op_recv.at[b], {"lat": lat, "lon": partner}
        )
        copy.wait_recv()
        copy.start()
        forwards.append(copy)

    total[...] = jnp.zeros_like(total)
    a, c3 = 0.7978845608028654, 0.044715

    def ahead(q, carry):
        r = q * 2
        pre = nn(pwt[...], jnp.concatenate([mixed[r], mixed[r + 1]], axis=1))
        square = pre * pre
        t = jnp.tanh(a * (pre + c3 * (square * pre)))
        gate = 0.5 * (1.0 + t)
        slope = gate + (0.5 * pre) * (1.0 - t * t) * (a * (1.0 + (3.0 * c3) * square))
        grid_f[r] = slope[:, :breadth]
        grid_f[r + 1] = slope[:, breadth:]
        here = jnp.concatenate([x1[r + 3], x1[r + 4]], axis=1).astype(F32)
        analysis = (here + pre * gate).astype(BF)
        total[...] += nt(jnp.concatenate([wt[r], wt[r + 1]], axis=1), analysis)
        return carry

    lax.fori_loop(0, height // 2, ahead, 0)
    prof[...] = nn(p_mat[...], total[...].astype(BF)).astype(BF)

    for j in range(half):
        b = lax.rem(partner + 2 * j, lons)
        remote(
            ops.at[b], ops.at[b], op_send.at[0], op_recv.at[b], {"lat": lat, "lon": partner}
        ).wait_recv()

    def instrument(o, carry):
        at = pl.ds(pl.multiple_of(o * CAP, CAP), CAP)
        hw = ops[o, :channels, :]
        lw = ops[o, channels : channels + levels, :]
        err = ops[o, err_row : err_row + 1, :levels].astype(F32)
        squashed = jnp.tanh(nn(prof[at, :], hw))
        misfit = nt(squashed.astype(BF), lw) - obs_slot[at, :].astype(F32)
        mis[at, :] = misfit.astype(BF)
        back = nn((err * misfit).astype(BF), lw) * (1.0 - squashed * squashed)
        adj[at, :] = nt(back.astype(BF), hw).astype(BF)
        return carry

    lax.fori_loop(0, lons, instrument, 0, unroll=4)
    dep_ref[...] = nn(pt_mat[...], mis[...]).T.astype(BF)
    adj_t = nn(pt_mat[...], adj[...]).T.astype(BF)

    def behind(q, carry):
        r = q * 2
        fb = nn(adj_t, jnp.concatenate([wt[r], wt[r + 1]], axis=1))
        gate = (fb * jnp.concatenate([grid_f[r], grid_f[r + 1]], axis=1)).astype(BF)
        grid_f[r] = fb[:, :breadth]
        grid_f[r + 1] = fb[:, breadth:]
        mb = nn(pw_ref[...], gate).astype(BF)
        x2[r + 3] = mb[:, :breadth]
        x2[r + 4] = mb[:, breadth:]
        return carry

    lax.fori_loop(0, height // 2, behind, 0)
    for copy in sends + forwards:
        copy.wait_send()
    make_edges(x2, edge.at[1])
    start_exchange(x2, *wires(1), send.at[1], recv.at[1], lats, lons)
    end_exchange(x2, *wires(1), halo, send.at[1], recv.at[1], lats, lons)

    def group_back(g, carry):
        base = pl.multiple_of(g * 16, 16)
        for i, v in enumerate(conv_group(x2, halo, taps, base, True)):
            stage[:, i, :] = v + grid_f[i, pl.ds(base, 16), :]
        out_ref[pl.ds(base, 16)] = stage[...].astype(BF)
        return carry

    lax.fori_loop(0, channels // 16, group_back, 0)


def body(
    state,
    depth_kernel,
    point_weight,
    column_index,
    column_weight,
    owner,
    observed,
    hidden_weight,
    level_weight,
    inverse_error,
):
    channels, height, breadth = state.shape
    obs, levels = observed.shape
    hid = hidden_weight.shape[2]
    lats, n = lax.axis_size("lat"), lax.axis_size("lon")
    slots = n * CAP
    depth = channels + levels + (-(channels + levels)) % 16 + 16
    args = (
        state,
        hidden_weight,
        level_weight.transpose(0, 2, 1),
        inverse_error,
        owner.T,
        column_index.T,
        column_weight.T,
        observed.T,
        depth_kernel.transpose(1, 2, 0),
        point_weight,
    )
    rows = height + 6
    grid = (rows, channels, breadth)
    vm = pltpu.VMEM
    grad, departures = pl.pallas_call(
        lambda *refs: kernel(lats, n, *refs),
        out_shape=(
            jax.ShapeDtypeStruct((channels, height, breadth), BF),
            jax.ShapeDtypeStruct((levels, obs), BF),
        ),
        in_specs=[VM] * len(args),
        out_specs=(VM, VM),
        scratch_shapes=[
            vm(grid, BF),
            vm(grid, BF),
            vm((16, height, breadth), F32),
            vm((8, obs), F32),
            vm((64, channels), F32),
            vm((channels, 64), F32),
            vm((channels, channels), BF),
            vm(grid, BF),
            vm((2, height, 8, channels), BF),
            vm((2, rows, 8, channels), BF),
            vm((2, rows, 8, channels), BF),
            vm((n, depth, hid), BF),
            vm((height, obs, breadth), BF),
            vm((slots, obs), BF),
            vm((obs, slots), BF),
            vm((slots, levels), BF),
            vm((height, channels, breadth), BF),
            vm((height, channels, breadth), F32),
            vm((obs, channels), F32),
            vm((slots, channels), BF),
            vm((slots, channels), BF),
            vm((slots, levels), BF),
            pltpu.SemaphoreType.DMA((2, 8)),
            pltpu.SemaphoreType.DMA((2, 8)),
            pltpu.SemaphoreType.DMA((n,)),
            pltpu.SemaphoreType.DMA((n,)),
        ],
        compiler_params=pltpu.CompilerParams(
            vmem_limit_bytes=56 << 20, collective_id=0, has_side_effects=True
        ),
    )(*args)
    return (grad, departures.T)


def solution(mesh):
    in_specs = (
        P(None, "lat", "lon"),
        P(),
        P(),
        P(("lat", "lon"), None),
        P(("lat", "lon"), None),
        P(("lat", "lon"), None),
        P(("lat", "lon"), None),
        P("lon", None, None),
        P("lon", None, None),
        P("lon", None),
    )
    out_specs = (P(None, "lat", "lon"), P(("lat", "lon"), None))
    return jax.shard_map(body, mesh=mesh, in_specs=in_specs, out_specs=out_specs, check_vma=False)
```

profile of v0, /device:TPU:1, one launch (start us, length us, event | category | flops | bytes accessed | tf_op | source)
XLA Modules:
  0.0 58.2 jit_solution(12592242751947015390)
XLA Ops:
  0.6 54.7 %shard_map.113 = (bf16[192,16,128]{2,1,0:T(8,128)(2,1)}, bf16[137,512]{1,0:T(8,128)(2,1)}) custom-call(bf16[192,16,128]{2,1,0:T(8,128)(2,1)} %refs_0_.1, bf16[1,192,512]{2,1,0:T(8,128)(2,1)} %refs_1_.1, bf16[1,137,512]{2,1,0:T(8,128)(2,1)} %bitcast.7, bf16[1,137]{1,0:T(2,128)(2,1)} %refs_3_.1, s32[1,512]{1,0:T(1,128)} %bitcast.13, s32[4,512]{1,0:T(4,128)} %bitcast.11, ...), custom_call_target="tpu_custom_call" | custom-call | tf_op jit(solution)/shard_map/pallas_call | solution.py:431
  55.3 0.0 copy-start
  55.3 2.2 %copy.14 = bf16[192,16,128]{2,1,0:T(8,128)(2,1)} copy(bf16[192,16,128]{2,1,0:T(8,128)(2,1)} %get-tuple-element.8) | data formatting | bytes 1572864
  57.5 0.0 copy-done
  57.5 0.7 %copy.15 = bf16[512,137]{0,1:T(8,128)(2,1)} copy(bf16[512,137]{0,1:T(8,128)(2,1)S(1)} %bitcast.9) | data formatting | bytes 280576
Async XLA Ops:
  55.3 2.2 %copy-start = (bf16[137,512]{1,0:T(8,128)(2,1)S(1)}, bf16[137,512]{1,0:T(8,128)(2,1)}, u32[]{:S(2)}) copy-start(bf16[137,512]{1,0:T(8,128)(2,1)} %get-tuple-element.5) | copy-start | bytes 420868
where the time goes:
time: 58.4 us; the launch traced here: 58.2 us
  Pallas kernels  54.7 us (94%)
  local copies, waits for them, and re-layouts  2.85 us (5%)
  between operations  0.65 us (1%)
    pallas_call x1, Pallas kernels, body(): pl.pallas_call(lambda *refs: kernel(lats, n, *refs), out_shape=(jax.Shape...  54.7 us
    unnamed x4, local copies, waits for them, and re-layouts  2.85 us

commit v1 on v0

--- a/solution.py
+++ b/solution.py
@@ -19,35 +19,138 @@
     return lax.dot_general(a, b, (((1,), (1,)), ((), ())), preferred_element_type=F32)
 
 
-def conv_group(x_ref, h_ref, k_ref, base, flip):
-    rows = x_ref.shape[0]
-    breadth = x_ref.shape[2]
+def flip_bit(q, bit):
+    return q + bit * (1 - 2 * lax.rem(q // bit, 2))
+
+
+def shifted(v, shift):
+    breadth = v.shape[1]
+    if not shift:
+        return v
+    lane = lax.broadcasted_iota(jnp.int32, v.shape, 1)
+    keep = lane < breadth - shift if shift > 0 else lane >= -shift
+    return jnp.where(keep, pltpu.roll(v, (-shift) % breadth, 1), jnp.zeros_like(v))
+
+
+def build_rows(taps, flip, height, breadth, a_ref):
+    depth, width = taps.shape[1], 2 * breadth
+    lane = lax.broadcasted_iota(jnp.int32, (1, width), 1)
+    tap = lax.broadcasted_iota(jnp.int32, (depth, width), 0)
+    own_col, own_row = lane // height, lane % height
+    q = lane - breadth
+    edge_col, k = q // 8, q % 8
+    edge_row = jnp.where(k < 4, k - 3, height + k - 4)
+    is_own = lane < 7 * height
+    is_edge = (q >= 0) & (q < 56) & (k != 3) & (k != 7)
+    col = jnp.where(is_own, own_col, edge_col)
+    row = jnp.where(is_own, own_row, edge_row)
+
+    def one(i, carry):
+        a = row - i + 3
+        good = (is_own | is_edge) & (a >= 0) & (a < 7)
+        want = (6 - a) * 8 + 6 - col if flip else a * 8 + col
+        want = jnp.where(good, want, -1)
+        pick = jnp.where(tap == want, 1.0, 0.0).astype(BF)
+        rows = nn(taps, pick)
+        for t in range(2):
+            a_ref[t, pl.ds(i, taps.shape[0], stride=height), :] = rows[
+                :, t * breadth : (t + 1) * breadth
+            ]
+        return carry
+
+    lax.fori_loop(0, height, one, 0)
+
+
+def side_weights(k_ref, flip, w_ref):
+    channels = k_ref.shape[2]
+    slot = lax.broadcasted_iota(jnp.int32, (8, channels), 0)
+    for a in range(7):
+        taps = k_ref[6 - a if flip else a].astype(F32)
+        for d in range(3):
+            r, l = (d, 6 - d) if flip else (6 - d, d)
+            right = jnp.where(slot >= 5 + d, jnp.broadcast_to(taps[r : r + 1], slot.shape), 0.0)
+            left = jnp.where(slot <= 2 - d, jnp.broadcast_to(taps[l : l + 1], slot.shape), 0.0)
+            w_ref[a * 3 + d] = right + left
+
+
+def conv_own(load, a_ref, out, height, breadth, count):
+    def pair(p, carry):
+        at = pl.ds(pl.multiple_of(p * 2 * height, 2 * height), 2 * height)
+        both = load(p, at)
+        cols = [
+            jnp.concatenate([shifted(v, b - 3) for b in range(7)], axis=0) for v in both
+        ]
+        lhs = a_ref[0, at, : 7 * height].astype(BF)
+        got = nn(lhs, jnp.concatenate(cols, axis=1))
+        for e in range(2):
+            rows = pl.ds(pl.multiple_of((p * 2 + e) * height, height), height)
+            out[rows, :] = got[e * height : (e + 1) * height, e * breadth : (e + 1) * breadth]
+        return carry
+
+    lax.fori_loop(0, count, pair, 0, unroll=4)
+
+
+def conv_edge(hal, a_ref, p, height, breadth):
+    cols = []
+    for e in range(2):
+        v = hal[pl.ds(pl.multiple_of((p * 2 + e) * 8, 8), 8), :]
+        cols.append(
+            jnp.concatenate([shifted(v, b - 3) for b in range(7)], axis=0).astype(BF)
+        )
+    at = pl.ds(pl.multiple_of(p * 2 * height, 2 * height), 2 * height)
+    lhs = a_ref[1, at, :56].astype(BF)
+    got = nn(lhs, jnp.concatenate(cols, axis=1))
+    return [
+        got[e * height : (e + 1) * height, e * breadth : (e + 1) * breadth] for e in range(2)
+    ]
+
+
+def side_sum(right_in, left_in, w_ref, m_ref, c_ref, ct_ref):
+    rows, _, channels = right_in.shape
     height = rows - 6
-    lane = lax.broadcasted_iota(jnp.int32, (16, breadth), 1)
-    taps = k_ref[pl.ds(base, 16), :]
-    acc = [None] * height
-    for col in range(7):
-        shift = col - 3
-        weights = []
-        for row in range(7):
-            t = (6 - row) * 8 + 6 - col if flip else row * 8 + col
-            weights.append(jnp.broadcast_to(taps[:, t : t + 1], (16, breadth)))
-        for r in range(rows):
-            v = x_ref[r, pl.ds(base, 16), :].astype(F32)
-            if shift:
-                edge = h_ref[r, pl.ds(base, 16), :].astype(F32)
-                mask = lane < shift if shift > 0 else lane >= breadth + shift
-                v = pltpu.roll(jnp.where(mask, edge, v), (-shift) % breadth, 1)
-            for row in range(7):
-                i = r - row
-                if 0 <= i < height:
-                    term = weights[row] * v
-                    acc[i] = term if acc[i] is None else acc[i] + term
-    return acc
-
-
-def prepare(owner, index, weight, obs_t, meta, wt_ref, p_ref, pt_ref, obs_slot):
-    height, obs, breadth = wt_ref.shape
+    slot = lax.broadcasted_iota(jnp.int32, (8, channels), 0)
+
+    def turn(r, carry):
+        both = jnp.where(slot < 4, right_in[r].astype(F32), left_in[r].astype(F32))
+        for d in range(3):
+            m_ref[d, r] = jnp.where(
+                slot >= 5, pltpu.roll(both, 5 + d, 0), pltpu.roll(both, 3 - d, 0)
+            )
+        return carry
+
+    lax.fori_loop(0, rows, turn, 0, unroll=2)
+
+    def group(g, carry):
+        acc = [jnp.zeros((8, channels), F32) for _ in range(4)]
+        for d in range(3):
+            for a in range(7):
+                w = w_ref[a * 3 + d]
+                for i in range(4):
+                    acc[i] = acc[i] + w * m_ref[d, g * 4 + i + a]
+        for i in range(4):
+            c_ref[pl.ds(pl.multiple_of((g * 4 + i) * 8, 8), 8), :] = acc[i]
+        return carry
+
+    lax.fori_loop(0, height // 4, group, 0)
+    ct_ref[...] = c_ref[...].T.astype(BF)
+
+
+def side_place(i, height, breadth):
+    part = lax.broadcasted_iota(jnp.int32, (8 * height, breadth), 0)
+    lane = lax.broadcasted_iota(jnp.int32, (8 * height, breadth), 1)
+    s = part - i * 8
+    hit = ((s >= 0) & (s < 3) & (lane == s)) | ((s > 4) & (s < 8) & (lane == s + breadth - 8))
+    return jnp.where(hit, 1.0, 0.0).astype(BF)
+
+
+def take_rows(lat_in, hal, channels):
+    for t in range(2):
+        for k in range(3):
+            hal[pl.ds(4 * t + k, channels, stride=8), :] = lat_in[t, k].astype(F32)
+
+
+def prepare(owner, index, weight, obs_t, meta, wt_ref, p_ref, pt_ref, obs_slot, height, breadth):
+    obs = wt_ref.shape[0]
     slots = p_ref.shape[0]
     n = slots // CAP
     si = lax.broadcasted_iota(jnp.int32, (obs, obs), 0)
@@ -76,7 +179,7 @@
     top = jnp.where(first, w[:, 0:1], jnp.where(second, w[:, 1:2], zero))
     bottom = jnp.where(first, w[:, 2:3], jnp.where(second, w[:, 3:4], zero))
     for r in range(height):
-        wt_ref[r] = jnp.where(r0 == r, top, jnp.where(r0 == r - 1, bottom, zero)).astype(BF)
+        wt_ref[:, r * breadth : (r + 1) * breadth] = jnp.where(r0 == r, top, jnp.where(r0 == r - 1, bottom, zero)).astype(BF)
     place = lax.broadcasted_iota(jnp.int32, (slots, obs), 0) == slot_row
     p = jnp.where(place, 1.0, 0.0).astype(BF)
     p_ref[...] = p
@@ -104,7 +207,7 @@
     return jnp.where(near | far, 1.0, 0.0).astype(BF)
 
 
-def copies(src, off, x, edge, right_in, left_in, send, recv, lats, lons):
+def copies(lat_out, lat_in, edge, right_in, left_in, send, recv, lats, lons):
     height = edge.shape[0]
     lat, lon = lax.axis_index("lat"), lax.axis_index("lon")
     left, right = lax.rem(lon + lons - 1, lons), lax.rem(lon + 1, lons)
@@ -120,32 +223,22 @@
     ]
     u, d = lax.max(lat - 1, 0), lax.min(lat + 1, lats - 1)
     up = [
-        make(0, src.at[pl.ds(off, 3)], x.at[high], {"lat": u, "lon": lon}),
+        make(0, lat_out.at[0], lat_in.at[1], {"lat": u, "lon": lon}),
         make(4, edge.at[low], right_in.at[high], {"lat": u, "lon": left}),
         make(5, edge.at[low], left_in.at[high], {"lat": u, "lon": right}),
     ]
     down = [
-        make(1, src.at[pl.ds(off + height - 3, 3)], x.at[low], {"lat": d, "lon": lon}),
+        make(1, lat_out.at[1], lat_in.at[0], {"lat": d, "lon": lon}),
         make(6, edge.at[end], right_in.at[low], {"lat": d, "lon": left}),
         make(7, edge.at[end], left_in.at[low], {"lat": d, "lon": right}),
     ]
     return lat > 0, lat < lats - 1, up, down, side
 
 
-def make_edges(src, edge):
-    pick = selector(src.shape[2])
-
-    def row(r, carry):
-        edge[r] = nt(pick, src[3 + r]).astype(BF)
-        return carry
-
-    lax.fori_loop(0, edge.shape[0], row, 0, unroll=4)
-
-
-def start_exchange(x, edge, right_in, left_in, send, recv, lats, lons):
+def start_lat(lat_out, lat_in, edge, right_in, left_in, send, recv, lats, lons):
     height = edge.shape[0]
     has_up, has_down, up, down, side = copies(
-        x, 3, x, edge, right_in, left_in, send, recv, lats, lons
+        lat_out, lat_in, edge, right_in, left_in, send, recv, lats, lons
     )
 
     @pl.when(has_up)
@@ -158,20 +251,22 @@
         for copy in down:
             copy.start()
 
-    for copy in side:
-        copy.start()
-    for has, at in ((has_up, 0), (has_down, height + 3)):
+    for has, t, at in ((has_up, 0, 0), (has_down, 1, height + 3)):
 
         @pl.when(jnp.logical_not(has))
         def _():
-            for ref in (x, right_in, left_in):
+            lat_in[t] = jnp.zeros(lat_in.shape[1:], BF)
+            for ref in (right_in, left_in):
                 ref[at : at + 3] = jnp.zeros((3,) + ref.shape[1:], BF)
 
 
-def end_exchange(x, edge, right_in, left_in, halo, send, recv, lats, lons):
-    has_up, has_down, up, down, side = copies(
-        x, 3, x, edge, right_in, left_in, send, recv, lats, lons
-    )
+def start_side(*refs):
+    for copy in copies(*refs)[4]:
+        copy.start()
+
+
+def end_exchange(*refs):
+    has_up, has_down, up, down, side = copies(*refs)
 
     @pl.when(has_up)
     def _():
@@ -189,15 +284,6 @@
 
     for copy in side:
         copy.wait()
-    pick = selector(x.shape[2])
-    near = lax.broadcasted_iota(jnp.int32, (8, x.shape[1]), 0) < 4
-
-    def row(r, carry):
-        both = jnp.where(near, right_in[r].astype(F32), left_in[r].astype(F32))
-        halo[r] = nn(both.T.astype(BF), pick).astype(BF)
-        return carry
-
-    lax.fori_loop(0, x.shape[0], row, 0, unroll=2)
 
 
 def kernel(
@@ -215,14 +301,23 @@
     pw_ref,
     out_ref,
     dep_ref,
-    x1,
-    x2,
-    stage,
+    cells,
+    back,
+    part,
+    a1,
+    a2,
+    w1,
+    w2,
+    m_sc,
+    c_sc,
+    ct_sc,
+    hal,
+    lat_out,
+    lat_in,
     meta,
     tap_rows,
     taps,
     pwt,
-    halo,
     edge,
     right_in,
     left_in,
@@ -231,9 +326,8 @@
     p_mat,
     pt_mat,
     obs_slot,
-    mixed,
     grid_f,
-    total,
+    ana,
     prof,
     adj,
     mis,
@@ -273,26 +367,43 @@
         for b in (partner, lon, other):
             greet(lat + 1, b)
 
-    def turn(g, carry):
-        at = pl.ds(pl.multiple_of(g * 16, 16), 16)
-        stage[...] = state[at].astype(F32)
-        for r in range(height):
-            x1[3 + r, at, :] = stage[:, r, :].astype(BF)
-        return carry
-
-    lax.fori_loop(0, channels // 16, turn, 0)
+    cells[...] = state[...].reshape(channels * height, breadth).astype(F32)
 
     def wires(k):
-        return edge.at[k], right_in.at[k], left_in.at[k]
-
-    make_edges(x1, edge.at[0])
+        return (
+            lat_out.at[k],
+            lat_in.at[k],
+            edge.at[k],
+            right_in.at[k],
+            left_in.at[k],
+            send.at[k],
+            recv.at[k],
+            lats,
+            lons,
+        )
+
+    def row_of(ref, r):
+        return ref[pl.ds(r, channels, stride=height), :]
+
+    pick = selector(breadth)
+
+    def edge_row(r, carry):
+        edge[0, r] = nt(pick, row_of(cells, r).astype(BF)).astype(BF)
+        return carry
+
+    lax.fori_loop(0, height, edge_row, 0, unroll=4)
+    for k in range(3):
+        lat_out[0, 0, k] = row_of(cells, k).astype(BF)
+        lat_out[0, 1, k] = row_of(cells, height - 3 + k).astype(BF)
+    hal[...] = jnp.zeros_like(hal)
     ops[lon] = jnp.zeros(ops.shape[1:], BF)
     ops[lon, :channels, :] = hw_ref[0]
     ops[lon, channels : channels + levels, :] = lw_ref[0]
     ops[lon, err_row : err_row + 1, :levels] = err_ref[...]
     sides = lax.min(lat, 1) + lax.min(lats - 1 - lat, 1)
     pl.semaphore_wait(barrier, half + 1 + 3 * sides)
-    start_exchange(x1, *wires(0), send.at[0], recv.at[0], lats, lons)
+    start_lat(*wires(0))
+    start_side(*wires(0))
     mine = ops.at[lon]
     sends = [
         remote(mine, mine, op_send.at[j], op_recv.at[lon], {"lat": lat, "lon": b})
@@ -303,18 +414,29 @@
     tap_rows[...] = jnp.zeros_like(tap_rows)
     for row in range(7):
         tap_rows[8 * row : 8 * row + 7, :] = k_ref[row].astype(F32)
-    taps[...] = tap_rows[...].T
+    taps[...] = tap_rows[...].T.astype(BF)
+    build_rows(taps[...], False, height, breadth, a1)
     pwt[...] = pw_ref[...].astype(F32).T.astype(BF)
-    prepare(owner, index, weight, obs_t, meta, wt, p_mat, pt_mat, obs_slot)
-    end_exchange(x1, *wires(0), halo, send.at[0], recv.at[0], lats, lons)
-
-    def group(g, carry):
-        base = pl.multiple_of(g * 16, 16)
-        for i, v in enumerate(conv_group(x1, halo, taps, base, False)):
-            mixed[i, pl.ds(base, 16), :] = v.astype(BF)
-        return carry
-
-    lax.fori_loop(0, channels // 16, group, 0)
+
+    def own_state(p, at):
+        return [state[2 * p], state[2 * p + 1]]
+
+    conv_own(own_state, a1, part, height, breadth, channels // 2)
+    side_weights(k_ref, False, w1)
+    prepare(
+        owner, index, weight, obs_t, meta, wt, p_mat, pt_mat, obs_slot, height, breadth
+    )
+    end_exchange(*wires(0))
+    take_rows(lat_in.at[0], hal, channels)
+    side_sum(right_in.at[0], left_in.at[0], w1, m_sc, c_sc, ct_sc)
+
+    def add_edge(p, carry):
+        for e, got in enumerate(conv_edge(hal, a1, p, height, breadth)):
+            at = pl.ds(pl.multiple_of((p * 2 + e) * height, height), height)
+            part[at, :] = part[at, :] + got
+        return carry
+
+    lax.fori_loop(0, channels // 2, add_edge, 0, unroll=4)
 
     forwards = []
     for j, b in enumerate(peers):
@@ -325,25 +447,29 @@
         copy.start()
         forwards.append(copy)
 
-    total[...] = jnp.zeros_like(total)
+    build_rows(taps[...], True, height, breadth, a2)
+    side_weights(k_ref, True, w2)
     a, c3 = 0.7978845608028654, 0.044715
 
     def ahead(q, carry):
         r = q * 2
-        pre = nn(pwt[...], jnp.concatenate([mixed[r], mixed[r + 1]], axis=1))
+        place = [side_place(r + t, height, breadth) for t in range(2)]
+        side = nn(ct_sc[...], jnp.concatenate(place, axis=1))
+        mixed = jnp.concatenate([row_of(part, r), row_of(part, r + 1)], axis=1) + side
+        pre = nn(pwt[...], mixed.astype(BF))
         square = pre * pre
         t = jnp.tanh(a * (pre + c3 * (square * pre)))
         gate = 0.5 * (1.0 + t)
         slope = gate + (0.5 * pre) * (1.0 - t * t) * (a * (1.0 + (3.0 * c3) * square))
-        grid_f[r] = slope[:, :breadth]
-        grid_f[r + 1] = slope[:, breadth:]
-        here = jnp.concatenate([x1[r + 3], x1[r + 4]], axis=1).astype(F32)
-        analysis = (here + pre * gate).astype(BF)
-        total[...] += nt(jnp.concatenate([wt[r], wt[r + 1]], axis=1), analysis)
-        return carry
-
-    lax.fori_loop(0, height // 2, ahead, 0)
-    prof[...] = nn(p_mat[...], total[...].astype(BF)).astype(BF)
+        two = pl.ds(pl.multiple_of(q * 2 * breadth, 2 * breadth), 2 * breadth)
+        grid_f[:, two] = slope
+        here = jnp.concatenate([row_of(cells, r), row_of(cells, r + 1)], axis=1)
+        ana[:, two] = (here + pre * gate).astype(BF)
+        return carry
+
+    lax.fori_loop(0, height // 2, ahead, 0, unroll=2)
+    total = nt(wt[...], ana[...])
+    prof[...] = nn(p_mat[...], total.astype(BF)).astype(BF)
 
     for j in range(half):
         b = lax.rem(partner + 2 * j, lons)
@@ -369,30 +495,59 @@
 
     def behind(q, carry):
         r = q * 2
-        fb = nn(adj_t, jnp.concatenate([wt[r], wt[r + 1]], axis=1))
-        gate = (fb * jnp.concatenate([grid_f[r], grid_f[r + 1]], axis=1)).astype(BF)
-        grid_f[r] = fb[:, :breadth]
-        grid_f[r + 1] = fb[:, breadth:]
-        mb = nn(pw_ref[...], gate).astype(BF)
-        x2[r + 3] = mb[:, :breadth]
-        x2[r + 4] = mb[:, breadth:]
-        return carry
-
-    lax.fori_loop(0, height // 2, behind, 0)
+        two = pl.ds(pl.multiple_of(q * 2 * breadth, 2 * breadth), 2 * breadth)
+        fb = nn(adj_t, wt[:, two])
+        gate = (fb * grid_f[:, two]).astype(BF)
+        grid_f[:, two] = fb
+        mb = nn(pw_ref[...], gate)
+        for t in range(2):
+            mine = mb[:, t * breadth : (t + 1) * breadth]
+            back[pl.ds(r + t, channels, stride=height), :] = mine
+            edge[1, r + t] = nt(pick, mine.astype(BF)).astype(BF)
+        return carry
+
+    last = height // 2
+    lax.fori_loop(0, 2, behind, 0, unroll=2)
+    lax.fori_loop(last - 2, last, behind, 0, unroll=2)
+    for k in range(3):
+        lat_out[1, 0, k] = row_of(back, k).astype(BF)
+        lat_out[1, 1, k] = row_of(back, height - 3 + k).astype(BF)
+    start_lat(*wires(1))
+    lax.fori_loop(2, last - 2, behind, 0, unroll=2)
+    start_side(*wires(1))
+
+    def own_back(p, at):
+        both = back[at, :].astype(BF)
+        return [both[:height], both[height:]]
+
+    conv_own(own_back, a2, part, height, breadth, channels // 2)
     for copy in sends + forwards:
         copy.wait_send()
-    make_edges(x2, edge.at[1])
-    start_exchange(x2, *wires(1), send.at[1], recv.at[1], lats, lons)
-    end_exchange(x2, *wires(1), halo, send.at[1], recv.at[1], lats, lons)
-
-    def group_back(g, carry):
-        base = pl.multiple_of(g * 16, 16)
-        for i, v in enumerate(conv_group(x2, halo, taps, base, True)):
-            stage[:, i, :] = v + grid_f[i, pl.ds(base, 16), :]
-        out_ref[pl.ds(base, 16)] = stage[...].astype(BF)
-        return carry
-
-    lax.fori_loop(0, channels // 16, group_back, 0)
+    end_exchange(*wires(1))
+    take_rows(lat_in.at[1], hal, channels)
+    side_sum(right_in.at[1], left_in.at[1], w2, m_sc, c_sc, ct_sc)
+
+    def add_side(q, carry):
+        r = q * 2
+        two = pl.ds(pl.multiple_of(q * 2 * breadth, 2 * breadth), 2 * breadth)
+        place = [side_place(r + t, height, breadth) for t in range(2)]
+        side = nn(ct_sc[...], jnp.concatenate(place, axis=1)) + grid_f[:, two]
+        for t in range(2):
+            cells[pl.ds(r + t, channels, stride=height), :] = side[
+                :, t * breadth : (t + 1) * breadth
+            ]
+        return carry
+
+    lax.fori_loop(0, height // 2, add_side, 0, unroll=2)
+
+    def finish(p, carry):
+        for e, got in enumerate(conv_edge(hal, a2, p, height, breadth)):
+            c = p * 2 + e
+            at = pl.ds(pl.multiple_of(c * height, height), height)
+            out_ref[c] = (cells[at, :] + part[at, :] + got).astype(BF)
+        return carry
+
+    lax.fori_loop(0, channels // 2, finish, 0, unroll=4)
 
 
 def body(
@@ -426,7 +581,6 @@
         point_weight,
     )
     rows = height + 6
-    grid = (rows, channels, breadth)
     vm = pltpu.VMEM
     grad, departures = pl.pallas_call(
         lambda *refs: kernel(lats, n, *refs),
@@ -437,25 +591,33 @@
         in_specs=[VM] * len(args),
         out_specs=(VM, VM),
         scratch_shapes=[
-            vm(grid, BF),
-            vm(grid, BF),
-            vm((16, height, breadth), F32),
+            vm((channels * height, breadth), F32),
+            vm((channels * height, breadth), F32),
+            vm((channels * height, breadth), F32),
+            vm((2, channels * height, breadth), F32),
+            vm((2, channels * height, breadth), F32),
+            vm((21, 8, channels), F32),
+            vm((21, 8, channels), F32),
+            vm((3, rows, 8, channels), F32),
+            vm((8 * height, channels), F32),
+            vm((channels, 8 * height), BF),
+            vm((channels * 8, breadth), F32),
+            vm((2, 2, 3, channels, breadth), BF),
+            vm((2, 2, 3, channels, breadth), BF),
             vm((8, obs), F32),
             vm((64, channels), F32),
-            vm((channels, 64), F32),
+            vm((channels, 64), BF),
             vm((channels, channels), BF),
-            vm(grid, BF),
             vm((2, height, 8, channels), BF),
             vm((2, rows, 8, channels), BF),
             vm((2, rows, 8, channels), BF),
             vm((n, depth, hid), BF),
-            vm((height, obs, breadth), BF),
+            vm((obs, height * breadth), BF),
             vm((slots, obs), BF),
             vm((obs, slots), BF),
             vm((slots, levels), BF),
-            vm((height, channels, breadth), BF),
-            vm((height, channels, breadth), F32),
-            vm((obs, channels), F32),
+            vm((channels, height * breadth), F32),
+            vm((channels, height * breadth), BF),
             vm((slots, channels), BF),
             vm((slots, channels), BF),
             vm((slots, levels), BF),

time: 58.4 us -> 57.3 us (0.981)
  Pallas kernels: 54.7 us -> 53.3 us
    pallas_call x1, Pallas kernels: 54.7 us -> 53.3 us  [body(): pl.pallas_call(lambda *refs: kernel(lats, n, *refs), out_shape=(jax.Shape...]
where the time goes in v1:
time: 57.3 us; the launch traced here: 56.8 us
  Pallas kernels  53.3 us (93%)
  local copies, waits for them, and re-layouts  2.85 us (5%)
  between operations  0.65 us (1%)
    pallas_call x1, Pallas kernels, body(): pl.pallas_call(lambda *refs: kernel(lats, n, *refs), out_shape=(jax.Shape...  53.3 us
    unnamed x4, local copies, waits for them, and re-layouts  2.85 us

profile of v1, /device:TPU:1, one launch (start us, length us, event | category | flops | bytes accessed | tf_op | source)
XLA Modules:
  0.0 56.8 jit_solution(13804229486967393697)
XLA Ops:
  0.6 53.3 %shard_map.113 = (bf16[192,16,128]{2,1,0:T(8,128)(2,1)}, bf16[137,512]{1,0:T(8,128)(2,1)}) custom-call(bf16[192,16,128]{2,1,0:T(8,128)(2,1)} %refs_0_.1, bf16[1,192,512]{2,1,0:T(8,128)(2,1)} %refs_1_.1, bf16[1,137,512]{2,1,0:T(8,128)(2,1)} %bitcast.7, bf16[1,137]{1,0:T(2,128)(2,1)} %refs_3_.1, s32[1,512]{1,0:T(1,128)} %bitcast.13, s32[4,512]{1,0:T(4,128)} %bitcast.11, ...), custom_call_target="tpu_custom_call" | custom-call | tf_op jit(solution)/shard_map/pallas_call | solution.py:585
  53.9 0.0 copy-start
  53.9 2.2 %copy.14 = bf16[192,16,128]{2,1,0:T(8,128)(2,1)} copy(bf16[192,16,128]{2,1,0:T(8,128)(2,1)} %get-tuple-element.8) | data formatting | bytes 1572864
  56.1 0.0 copy-done
  56.1 0.7 %copy.15 = bf16[512,137]{0,1:T(8,128)(2,1)} copy(bf16[512,137]{0,1:T(8,128)(2,1)S(1)} %bitcast.9) | data formatting | bytes 280576
Async XLA Ops:
  53.9 2.2 %copy-start = (bf16[137,512]{1,0:T(8,128)(2,1)S(1)}, bf16[137,512]{1,0:T(8,128)(2,1)}, u32[]{:S(2)}) copy-start(bf16[137,512]{1,0:T(8,128)(2,1)} %get-tuple-element.5) | copy-start | bytes 420868

commit v2 on v1

--- a/solution.py
+++ b/solution.py
@@ -17,10 +17,6 @@
 
 def nt(a, b):
     return lax.dot_general(a, b, (((1,), (1,)), ((), ())), preferred_element_type=F32)
-
-
-def flip_bit(q, bit):
-    return q + bit * (1 - 2 * lax.rem(q // bit, 2))
 
 
 def shifted(v, shift):
@@ -30,35 +26,6 @@
     lane = lax.broadcasted_iota(jnp.int32, v.shape, 1)
     keep = lane < breadth - shift if shift > 0 else lane >= -shift
     return jnp.where(keep, pltpu.roll(v, (-shift) % breadth, 1), jnp.zeros_like(v))
-
-
-def build_rows(taps, flip, height, breadth, a_ref):
-    depth, width = taps.shape[1], 2 * breadth
-    lane = lax.broadcasted_iota(jnp.int32, (1, width), 1)
-    tap = lax.broadcasted_iota(jnp.int32, (depth, width), 0)
-    own_col, own_row = lane // height, lane % height
-    q = lane - breadth
-    edge_col, k = q // 8, q % 8
-    edge_row = jnp.where(k < 4, k - 3, height + k - 4)
-    is_own = lane < 7 * height
-    is_edge = (q >= 0) & (q < 56) & (k != 3) & (k != 7)
-    col = jnp.where(is_own, own_col, edge_col)
-    row = jnp.where(is_own, own_row, edge_row)
-
-    def one(i, carry):
-        a = row - i + 3
-        good = (is_own | is_edge) & (a >= 0) & (a < 7)
-        want = (6 - a) * 8 + 6 - col if flip else a * 8 + col
-        want = jnp.where(good, want, -1)
-        pick = jnp.where(tap == want, 1.0, 0.0).astype(BF)
-        rows = nn(taps, pick)
-        for t in range(2):
-            a_ref[t, pl.ds(i, taps.shape[0], stride=height), :] = rows[
-                :, t * breadth : (t + 1) * breadth
-            ]
-        return carry
-
-    lax.fori_loop(0, height, one, 0)
 
 
 def side_weights(k_ref, flip, w_ref):
@@ -73,36 +40,48 @@
             w_ref[a * 3 + d] = right + left
 
 
-def conv_own(load, a_ref, out, height, breadth, count):
-    def pair(p, carry):
-        at = pl.ds(pl.multiple_of(p * 2 * height, 2 * height), 2 * height)
-        both = load(p, at)
-        cols = [
-            jnp.concatenate([shifted(v, b - 3) for b in range(7)], axis=0) for v in both
-        ]
-        lhs = a_ref[0, at, : 7 * height].astype(BF)
-        got = nn(lhs, jnp.concatenate(cols, axis=1))
-        for e in range(2):
-            rows = pl.ds(pl.multiple_of((p * 2 + e) * height, height), height)
-            out[rows, :] = got[e * height : (e + 1) * height, e * breadth : (e + 1) * breadth]
-        return carry
-
-    lax.fori_loop(0, count, pair, 0, unroll=4)
-
-
-def conv_edge(hal, a_ref, p, height, breadth):
-    cols = []
-    for e in range(2):
-        v = hal[pl.ds(pl.multiple_of((p * 2 + e) * 8, 8), 8), :]
-        cols.append(
-            jnp.concatenate([shifted(v, b - 3) for b in range(7)], axis=0).astype(BF)
-        )
-    at = pl.ds(pl.multiple_of(p * 2 * height, 2 * height), 2 * height)
-    lhs = a_ref[1, at, :56].astype(BF)
-    got = nn(lhs, jnp.concatenate(cols, axis=1))
-    return [
-        got[e * height : (e + 1) * height, e * breadth : (e + 1) * breadth] for e in range(2)
-    ]
+def conv_own(x, out, weights, base):
+    height, _, breadth = x.shape
+    at = pl.ds(base, 16)
+    acc = [None] * height
+    for col in range(7):
+        w = weights(col)
+        part = [None] * height
+        for r in range(height):
+            v = shifted(x[r, at, :], col - 3)
+            for row in range(7):
+                i = r + 3 - row
+                if 0 <= i < height:
+                    term = w[row] * v
+                    part[i] = term if part[i] is None else part[i] + term
+            for i in range(height):
+                if part[i] is not None and r == min(i + 3, height - 1):
+                    whole = part[i].astype(F32)
+                    acc[i] = whole if acc[i] is None else acc[i] + whole
+                    part[i] = None
+    for i in range(height):
+        out[i, at, :] = acc[i]
+
+
+def conv_edge(lat_in, out, weights, base):
+    height = out.shape[0]
+    at = pl.ds(base, 16)
+    acc = {}
+    for col in range(7):
+        w = weights(col)
+        part = {}
+        for t in range(2):
+            for k in range(3):
+                v = shifted(lat_in[t, k, at, :], col - 3)
+                span = range(0, k + 1) if t == 0 else range(height - 3 + k, height)
+                for i in span:
+                    term = w[k - i if t == 0 else height + 3 + k - i] * v
+                    part[i] = part[i] + term if i in part else term
+        for i, v in part.items():
+            whole = v.astype(F32)
+            acc[i] = acc[i] + whole if i in acc else whole
+    for i, v in acc.items():
+        out[i, at, :] = out[i, at, :] + v
 
 
 def side_sum(right_in, left_in, w_ref, m_ref, c_ref, ct_ref):
@@ -141,12 +120,6 @@
     s = part - i * 8
     hit = ((s >= 0) & (s < 3) & (lane == s)) | ((s > 4) & (s < 8) & (lane == s + breadth - 8))
     return jnp.where(hit, 1.0, 0.0).astype(BF)
-
-
-def take_rows(lat_in, hal, channels):
-    for t in range(2):
-        for k in range(3):
-            hal[pl.ds(4 * t + k, channels, stride=8), :] = lat_in[t, k].astype(F32)
 
 
 def prepare(owner, index, weight, obs_t, meta, wt_ref, p_ref, pt_ref, obs_slot, height, breadth):
@@ -207,7 +180,7 @@
     return jnp.where(near | far, 1.0, 0.0).astype(BF)
 
 
-def copies(lat_out, lat_in, edge, right_in, left_in, send, recv, lats, lons):
+def copies(grid, lat_in, edge, right_in, left_in, send, recv, lats, lons):
     height = edge.shape[0]
     lat, lon = lax.axis_index("lat"), lax.axis_index("lon")
     left, right = lax.rem(lon + lons - 1, lons), lax.rem(lon + 1, lons)
@@ -223,22 +196,22 @@
     ]
     u, d = lax.max(lat - 1, 0), lax.min(lat + 1, lats - 1)
     up = [
-        make(0, lat_out.at[0], lat_in.at[1], {"lat": u, "lon": lon}),
+        make(0, grid.at[low], lat_in.at[1], {"lat": u, "lon": lon}),
         make(4, edge.at[low], right_in.at[high], {"lat": u, "lon": left}),
         make(5, edge.at[low], left_in.at[high], {"lat": u, "lon": right}),
     ]
     down = [
-        make(1, lat_out.at[1], lat_in.at[0], {"lat": d, "lon": lon}),
+        make(1, grid.at[end], lat_in.at[0], {"lat": d, "lon": lon}),
         make(6, edge.at[end], right_in.at[low], {"lat": d, "lon": left}),
         make(7, edge.at[end], left_in.at[low], {"lat": d, "lon": right}),
     ]
     return lat > 0, lat < lats - 1, up, down, side
 
 
-def start_lat(lat_out, lat_in, edge, right_in, left_in, send, recv, lats, lons):
+def start_lat(grid, lat_in, edge, right_in, left_in, send, recv, lats, lons):
     height = edge.shape[0]
     has_up, has_down, up, down, side = copies(
-        lat_out, lat_in, edge, right_in, left_in, send, recv, lats, lons
+        grid, lat_in, edge, right_in, left_in, send, recv, lats, lons
     )
 
     @pl.when(has_up)
@@ -302,17 +275,15 @@
     out_ref,
     dep_ref,
     cells,
-    back,
+    x1,
+    x2,
     part,
-    a1,
-    a2,
+    wide,
     w1,
     w2,
     m_sc,
     c_sc,
     ct_sc,
-    hal,
-    lat_out,
     lat_in,
     meta,
     tap_rows,
@@ -369,9 +340,11 @@
 
     cells[...] = state[...].reshape(channels * height, breadth).astype(F32)
 
+    grids = (x1, x2)
+
     def wires(k):
         return (
-            lat_out.at[k],
+            grids[k],
             lat_in.at[k],
             edge.at[k],
             right_in.at[k],
@@ -388,14 +361,12 @@
     pick = selector(breadth)
 
     def edge_row(r, carry):
-        edge[0, r] = nt(pick, row_of(cells, r).astype(BF)).astype(BF)
-        return carry
-
-    lax.fori_loop(0, height, edge_row, 0, unroll=4)
-    for k in range(3):
-        lat_out[0, 0, k] = row_of(cells, k).astype(BF)
-        lat_out[0, 1, k] = row_of(cells, height - 3 + k).astype(BF)
-    hal[...] = jnp.zeros_like(hal)
+        mine = row_of(cells, r).astype(BF)
+        x1[r] = mine
+        edge[0, r] = nt(pick, mine).astype(BF)
+        return carry
+
+    lax.fori_loop(0, height, edge_row, 0, unroll=8)
     ops[lon] = jnp.zeros(ops.shape[1:], BF)
     ops[lon, :channels, :] = hw_ref[0]
     ops[lon, channels : channels + levels, :] = lw_ref[0]
@@ -414,29 +385,45 @@
     tap_rows[...] = jnp.zeros_like(tap_rows)
     for row in range(7):
         tap_rows[8 * row : 8 * row + 7, :] = k_ref[row].astype(F32)
-    taps[...] = tap_rows[...].T.astype(BF)
-    build_rows(taps[...], False, height, breadth, a1)
+    taps[...] = tap_rows[...].T
     pwt[...] = pw_ref[...].astype(F32).T.astype(BF)
 
-    def own_state(p, at):
-        return [state[2 * p], state[2 * p + 1]]
-
-    conv_own(own_state, a1, part, height, breadth, channels // 2)
+    def group(g, carry):
+        base = pl.multiple_of(g * 16, 16)
+        local = taps[pl.ds(base, 16), :]
+
+        def spread(col):
+            out = []
+            for row in range(7):
+                t = row * 8 + col
+                w = jnp.broadcast_to(local[:, t : t + 1], (16, breadth)).astype(BF)
+                wide[g, row * 7 + col] = w
+                out.append(w)
+            return out
+
+        conv_own(x1, part, spread, base)
+        return carry
+
+    lax.fori_loop(0, channels // 16, group, 0)
+
+    def straight(g):
+        return lambda col: [wide[g, row * 7 + col] for row in range(7)]
+
+    def flipped(g):
+        return lambda col: [wide[g, (6 - row) * 7 + 6 - col] for row in range(7)]
+
     side_weights(k_ref, False, w1)
     prepare(
         owner, index, weight, obs_t, meta, wt, p_mat, pt_mat, obs_slot, height, breadth
     )
     end_exchange(*wires(0))
-    take_rows(lat_in.at[0], hal, channels)
     side_sum(right_in.at[0], left_in.at[0], w1, m_sc, c_sc, ct_sc)
 
-    def add_edge(p, carry):
-        for e, got in enumerate(conv_edge(hal, a1, p, height, breadth)):
-            at = pl.ds(pl.multiple_of((p * 2 + e) * height, height), height)
-            part[at, :] = part[at, :] + got
-        return carry
-
-    lax.fori_loop(0, channels // 2, add_edge, 0, unroll=4)
+    def add_edge(g, carry):
+        conv_edge(lat_in.at[0], part, straight(g), pl.multiple_of(g * 16, 16))
+        return carry
+
+    lax.fori_loop(0, channels // 16, add_edge, 0, unroll=2)
 
     forwards = []
     for j, b in enumerate(peers):
@@ -447,7 +434,6 @@
         copy.start()
         forwards.append(copy)
 
-    build_rows(taps[...], True, height, breadth, a2)
     side_weights(k_ref, True, w2)
     a, c3 = 0.7978845608028654, 0.044715
 
@@ -455,7 +441,7 @@
         r = q * 2
         place = [side_place(r + t, height, breadth) for t in range(2)]
         side = nn(ct_sc[...], jnp.concatenate(place, axis=1))
-        mixed = jnp.concatenate([row_of(part, r), row_of(part, r + 1)], axis=1) + side
+        mixed = jnp.concatenate([part[r], part[r + 1]], axis=1) + side
         pre = nn(pwt[...], mixed.astype(BF))
         square = pre * pre
         t = jnp.tanh(a * (pre + c3 * (square * pre)))
@@ -463,7 +449,7 @@
         slope = gate + (0.5 * pre) * (1.0 - t * t) * (a * (1.0 + (3.0 * c3) * square))
         two = pl.ds(pl.multiple_of(q * 2 * breadth, 2 * breadth), 2 * breadth)
         grid_f[:, two] = slope
-        here = jnp.concatenate([row_of(cells, r), row_of(cells, r + 1)], axis=1)
+        here = jnp.concatenate([x1[r], x1[r + 1]], axis=1).astype(F32)
         ana[:, two] = (here + pre * gate).astype(BF)
         return carry
 
@@ -499,33 +485,35 @@
         fb = nn(adj_t, wt[:, two])
         gate = (fb * grid_f[:, two]).astype(BF)
         grid_f[:, two] = fb
-        mb = nn(pw_ref[...], gate)
+        mb = nn(pw_ref[...], gate).astype(BF)
         for t in range(2):
             mine = mb[:, t * breadth : (t + 1) * breadth]
-            back[pl.ds(r + t, channels, stride=height), :] = mine
-            edge[1, r + t] = nt(pick, mine.astype(BF)).astype(BF)
+            x2[r + t] = mine
+            edge[1, r + t] = nt(pick, mine).astype(BF)
         return carry
 
     last = height // 2
     lax.fori_loop(0, 2, behind, 0, unroll=2)
     lax.fori_loop(last - 2, last, behind, 0, unroll=2)
-    for k in range(3):
-        lat_out[1, 0, k] = row_of(back, k).astype(BF)
-        lat_out[1, 1, k] = row_of(back, height - 3 + k).astype(BF)
     start_lat(*wires(1))
     lax.fori_loop(2, last - 2, behind, 0, unroll=2)
     start_side(*wires(1))
 
-    def own_back(p, at):
-        both = back[at, :].astype(BF)
-        return [both[:height], both[height:]]
-
-    conv_own(own_back, a2, part, height, breadth, channels // 2)
+    def group_back(g, carry):
+        conv_own(x2, part, flipped(g), pl.multiple_of(g * 16, 16))
+        return carry
+
+    lax.fori_loop(0, channels // 16, group_back, 0)
     for copy in sends + forwards:
         copy.wait_send()
     end_exchange(*wires(1))
-    take_rows(lat_in.at[1], hal, channels)
     side_sum(right_in.at[1], left_in.at[1], w2, m_sc, c_sc, ct_sc)
+
+    def edge_back(g, carry):
+        conv_edge(lat_in.at[1], part, flipped(g), pl.multiple_of(g * 16, 16))
+        return carry
+
+    lax.fori_loop(0, channels // 16, edge_back, 0, unroll=2)
 
     def add_side(q, carry):
         r = q * 2
@@ -533,21 +521,13 @@
         place = [side_place(r + t, height, breadth) for t in range(2)]
         side = nn(ct_sc[...], jnp.concatenate(place, axis=1)) + grid_f[:, two]
         for t in range(2):
-            cells[pl.ds(r + t, channels, stride=height), :] = side[
-                :, t * breadth : (t + 1) * breadth
-            ]
+            cells[pl.ds(r + t, channels, stride=height), :] = (
+                side[:, t * breadth : (t + 1) * breadth] + part[r + t]
+            )
         return carry
 
     lax.fori_loop(0, height // 2, add_side, 0, unroll=2)
-
-    def finish(p, carry):
-        for e, got in enumerate(conv_edge(hal, a2, p, height, breadth)):
-            c = p * 2 + e
-            at = pl.ds(pl.multiple_of(c * height, height), height)
-            out_ref[c] = (cells[at, :] + part[at, :] + got).astype(BF)
-        return carry
-
-    lax.fori_loop(0, channels // 2, finish, 0, unroll=4)
+    out_ref[...] = cells[...].astype(BF).reshape(out_ref.shape)
 
 
 def body(
@@ -592,21 +572,19 @@
         out_specs=(VM, VM),
         scratch_shapes=[
             vm((channels * height, breadth), F32),
-            vm((channels * height, breadth), F32),
-            vm((channels * height, breadth), F32),
-            vm((2, channels * height, breadth), F32),
-            vm((2, channels * height, breadth), F32),
+            vm((height, channels, breadth), BF),
+            vm((height, channels, breadth), BF),
+            vm((height, channels, breadth), F32),
+            vm((channels // 16, 49, 16, breadth), BF),
             vm((21, 8, channels), F32),
             vm((21, 8, channels), F32),
             vm((3, rows, 8, channels), F32),
             vm((8 * height, channels), F32),
             vm((channels, 8 * height), BF),
-            vm((channels * 8, breadth), F32),
-            vm((2, 2, 3, channels, breadth), BF),
             vm((2, 2, 3, channels, breadth), BF),
             vm((8, obs), F32),
             vm((64, channels), F32),
-            vm((channels, 64), BF),
+            vm((channels, 64), F32),
             vm((channels, channels), BF),
             vm((2, height, 8, channels), BF),
             vm((2, rows, 8, channels), BF),

time: 57.3 us -> 49.2 us (0.86)
  Pallas kernels: 53.3 us -> 45.2 us
    pallas_call x1, Pallas kernels: 53.3 us -> 45.2 us  [body(): pl.pallas_call(lambda *refs: kernel(lats, n, *refs), out_shape=(jax.Shape...]
where the time goes in v2:
time: 49.2 us; the launch traced here: 48.7 us
  Pallas kernels  45.2 us (92%)
  local copies, waits for them, and re-layouts  2.85 us (6%)
  between operations  0.65 us (1%)
    pallas_call x1, Pallas kernels, body(): pl.pallas_call(lambda *refs: kernel(lats, n, *refs), out_shape=(jax.Shape...  45.2 us
    unnamed x4, local copies, waits for them, and re-layouts  2.85 us

profile of v2, /device:TPU:1, one launch (start us, length us, event | category | flops | bytes accessed | tf_op | source)
XLA Modules:
  0.0 48.7 jit_solution(9758158639240234431)
XLA Ops:
  0.6 45.2 %shard_map.113 = (bf16[192,16,128]{2,1,0:T(8,128)(2,1)}, bf16[137,512]{1,0:T(8,128)(2,1)}) custom-call(bf16[192,16,128]{2,1,0:T(8,128)(2,1)} %refs_0_.1, bf16[1,192,512]{2,1,0:T(8,128)(2,1)} %refs_1_.1, bf16[1,137,512]{2,1,0:T(8,128)(2,1)} %bitcast.7, bf16[1,137]{1,0:T(2,128)(2,1)} %refs_3_.1, s32[1,512]{1,0:T(1,128)} %bitcast.13, s32[4,512]{1,0:T(4,128)} %bitcast.11, ...), custom_call_target="tpu_custom_call" | custom-call | tf_op jit(solution)/shard_map/pallas_call | solution.py:565
  45.8 0.0 copy-start
  45.8 2.2 %copy.14 = bf16[192,16,128]{2,1,0:T(8,128)(2,1)} copy(bf16[192,16,128]{2,1,0:T(8,128)(2,1)} %get-tuple-element.8) | data formatting | bytes 1572864
  48.0 0.0 copy-done
  48.0 0.7 %copy.15 = bf16[512,137]{0,1:T(8,128)(2,1)} copy(bf16[512,137]{0,1:T(8,128)(2,1)S(1)} %bitcast.9) | data formatting | bytes 280576
Async XLA Ops:
  45.8 2.2 %copy-start = (bf16[137,512]{1,0:T(8,128)(2,1)S(1)}, bf16[137,512]{1,0:T(8,128)(2,1)}, u32[]{:S(2)}) copy-start(bf16[137,512]{1,0:T(8,128)(2,1)} %get-tuple-element.5) | copy-start | bytes 420868

commit v3 on v2

--- a/solution.py
+++ b/solution.py
@@ -17,6 +17,10 @@
 
 def nt(a, b):
     return lax.dot_general(a, b, (((1,), (1,)), ((), ())), preferred_element_type=F32)
+
+
+def flip_bit(q, bit):
+    return q + bit * (1 - 2 * lax.rem(lax.div(q, bit), 2))
 
 
 def shifted(v, shift):
@@ -309,12 +313,26 @@
 ):
     channels, height, breadth = state.shape
     levels = obs_t.shape[0]
-    err_row = ops.shape[1] - 16
+    err_row = channels + levels
     lat, lon = lax.axis_index("lat"), lax.axis_index("lon")
     partner = lon + 1 - 2 * lax.rem(lon, 2)
     other = lax.rem(lon + lons - 1 + 2 * lax.rem(lon, 2), lons)
     half = lons // 2
-    peers = [lax.rem(lon + 2 * j, lons) for j in range(1, half)]
+    bits = half.bit_length() - 1
+    core, chip = lax.rem(lon, 2), lax.div(lon, 2)
+
+    def across(q, t, c):
+        first, second = flip_bit(q, 1 << t), flip_bit(q, 1 << (bits - 1 - t))
+        return first + c * (second - first)
+
+    def holder(mask, c):
+        q = chip
+        for t in range(bits):
+            if mask >> t & 1:
+                q = across(q, t, c)
+        return 2 * q + c
+
+    peers = [holder(1 << t, core) for t in range(bits)]
     barrier = pltpu.get_barrier_semaphore()
 
     def greet(a, b):
@@ -372,16 +390,27 @@
     ops[lon, channels : channels + levels, :] = lw_ref[0]
     ops[lon, err_row : err_row + 1, :levels] = err_ref[...]
     sides = lax.min(lat, 1) + lax.min(lats - 1 - lat, 1)
-    pl.semaphore_wait(barrier, half + 1 + 3 * sides)
+    pl.semaphore_wait(barrier, bits + 2 + 3 * sides)
     start_lat(*wires(0))
     start_side(*wires(0))
-    mine = ops.at[lon]
-    sends = [
-        remote(mine, mine, op_send.at[j], op_recv.at[lon], {"lat": lat, "lon": b})
-        for j, b in enumerate([partner] + peers)
-    ]
-    for copy in sends:
-        copy.start()
+    started = []
+
+    def op_copy(o, b):
+        return remote(
+            ops.at[o], ops.at[o], op_send.at[len(started)], op_recv.at[o], {"lat": lat, "lon": b}
+        )
+
+    def pass_on(mask):
+        o = holder(mask, core)
+        if mask:
+            op_copy(o, partner).wait_recv()
+        for t in range(mask.bit_length(), bits):
+            started.append(op_copy(o, peers[t]))
+            started[-1].start()
+        started.append(op_copy(o, partner))
+        started[-1].start()
+
+    pass_on(0)
     tap_rows[...] = jnp.zeros_like(tap_rows)
     for row in range(7):
         tap_rows[8 * row : 8 * row + 7, :] = k_ref[row].astype(F32)
@@ -424,15 +453,6 @@
         return carry
 
     lax.fori_loop(0, channels // 16, add_edge, 0, unroll=2)
-
-    forwards = []
-    for j, b in enumerate(peers):
-        copy = remote(
-            ops.at[b], ops.at[b], op_send.at[half + j], op_recv.at[b], {"lat": lat, "lon": partner}
-        )
-        copy.wait_recv()
-        copy.start()
-        forwards.append(copy)
 
     side_weights(k_ref, True, w2)
     a, c3 = 0.7978845608028654, 0.044715
@@ -454,16 +474,11 @@
         return carry
 
     lax.fori_loop(0, height // 2, ahead, 0, unroll=2)
+    pass_on(1)
     total = nt(wt[...], ana[...])
     prof[...] = nn(p_mat[...], total.astype(BF)).astype(BF)
 
-    for j in range(half):
-        b = lax.rem(partner + 2 * j, lons)
-        remote(
-            ops.at[b], ops.at[b], op_send.at[0], op_recv.at[b], {"lat": lat, "lon": partner}
-        ).wait_recv()
-
-    def instrument(o, carry):
+    def instrument(o):
         at = pl.ds(pl.multiple_of(o * CAP, CAP), CAP)
         hw = ops[o, :channels, :]
         lw = ops[o, channels : channels + levels, :]
@@ -473,9 +488,22 @@
         mis[at, :] = misfit.astype(BF)
         back = nn((err * misfit).astype(BF), lw) * (1.0 - squashed * squashed)
         adj[at, :] = nt(back.astype(BF), hw).astype(BF)
-        return carry
-
-    lax.fori_loop(0, lons, instrument, 0, unroll=4)
+
+    def from_partner(mask):
+        o = holder(mask, 1 - core)
+        op_copy(o, partner).wait_recv()
+        return o
+
+    for mask in range(2, half - 1):
+        pass_on(mask)
+    early = [lon, from_partner(0)] + [holder(mask, core) for mask in range(1, half - 1)]
+    for o in early:
+        instrument(o)
+    if half > 2:
+        pass_on(half - 1)
+    late = [from_partner(mask) for mask in range(1, half)]
+    for o in [holder(half - 1, core)] + late:
+        instrument(o)
     dep_ref[...] = nn(pt_mat[...], mis[...]).T.astype(BF)
     adj_t = nn(pt_mat[...], adj[...]).T.astype(BF)
 
@@ -504,7 +532,7 @@
         return carry
 
     lax.fori_loop(0, channels // 16, group_back, 0)
-    for copy in sends + forwards:
+    for copy in started:
         copy.wait_send()
     end_exchange(*wires(1))
     side_sum(right_in.at[1], left_in.at[1], w2, m_sc, c_sc, ct_sc)
@@ -547,7 +575,7 @@
     hid = hidden_weight.shape[2]
     lats, n = lax.axis_size("lat"), lax.axis_size("lon")
     slots = n * CAP
-    depth = channels + levels + (-(channels + levels)) % 16 + 16
+    depth = channels + levels + 1 + (-(channels + levels + 1)) % 16
     args = (
         state,
         hidden_weight,

time: 49.2 us -> 44.8 us (0.911)
  Pallas kernels: 45.2 us -> 41.1 us
    pallas_call x1, Pallas kernels: 45.2 us -> 41.1 us  [body(): pl.pallas_call(lambda *refs: kernel(lats, n, *refs), out_shape=(jax.Shape...]
where the time goes in v3:
time: 44.8 us; the launch traced here: 44.6 us
  Pallas kernels  41.1 us (92%)
  local copies, waits for them, and re-layouts  2.85 us (6%)
  between operations  0.65 us (1%)
    pallas_call x1, Pallas kernels, body(): pl.pallas_call(lambda *refs: kernel(lats, n, *refs), out_shape=(jax.Shape...  41.1 us
    unnamed x4, local copies, waits for them, and re-layouts  2.85 us

profile of v3, /device:TPU:1, one launch (start us, length us, event | category | flops | bytes accessed | tf_op | source)
XLA Modules:
  0.0 44.6 jit_solution(7866622853834414448)
XLA Ops:
  0.6 41.1 %shard_map.113 = (bf16[192,16,128]{2,1,0:T(8,128)(2,1)}, bf16[137,512]{1,0:T(8,128)(2,1)}) custom-call(bf16[192,16,128]{2,1,0:T(8,128)(2,1)} %refs_0_.1, bf16[1,192,512]{2,1,0:T(8,128)(2,1)} %refs_1_.1, bf16[1,137,512]{2,1,0:T(8,128)(2,1)} %bitcast.7, bf16[1,137]{1,0:T(2,128)(2,1)} %refs_3_.1, s32[1,512]{1,0:T(1,128)} %bitcast.13, s32[4,512]{1,0:T(4,128)} %bitcast.11, ...), custom_call_target="tpu_custom_call" | custom-call | tf_op jit(solution)/shard_map/pallas_call | solution.py:593
  41.8 0.0 copy-start
  41.8 2.2 %copy.14 = bf16[192,16,128]{2,1,0:T(8,128)(2,1)} copy(bf16[192,16,128]{2,1,0:T(8,128)(2,1)} %get-tuple-element.8) | data formatting | bytes 1572864
  44.0 0.0 copy-done
  44.0 0.7 %copy.15 = bf16[512,137]{0,1:T(8,128)(2,1)} copy(bf16[512,137]{0,1:T(8,128)(2,1)S(1)} %bitcast.9) | data formatting | bytes 280576
Async XLA Ops:
  41.8 2.2 %copy-start = (bf16[137,512]{1,0:T(8,128)(2,1)S(1)}, bf16[137,512]{1,0:T(8,128)(2,1)}, u32[]{:S(2)}) copy-start(bf16[137,512]{1,0:T(8,128)(2,1)} %get-tuple-element.5) | copy-start | bytes 420868

commit v4 on v3

--- a/solution.py
+++ b/solution.py
@@ -404,7 +404,7 @@
         o = holder(mask, core)
         if mask:
             op_copy(o, partner).wait_recv()
-        for t in range(mask.bit_length(), bits):
+        for t in range(mask.bit_length(), bits if mask else 1):
             started.append(op_copy(o, peers[t]))
             started[-1].start()
         started.append(op_copy(o, partner))
@@ -425,9 +425,9 @@
             out = []
             for row in range(7):
                 t = row * 8 + col
-                w = jnp.broadcast_to(local[:, t : t + 1], (16, breadth)).astype(BF)
+                w = jnp.broadcast_to(local[:, t : t + 1], (16, breadth))
                 wide[g, row * 7 + col] = w
-                out.append(w)
+                out.append(w.astype(BF))
             return out
 
         conv_own(x1, part, spread, base)
@@ -436,11 +436,14 @@
     lax.fori_loop(0, channels // 16, group, 0)
 
     def straight(g):
-        return lambda col: [wide[g, row * 7 + col] for row in range(7)]
+        return lambda col: [wide[g, row * 7 + col].astype(BF) for row in range(7)]
 
     def flipped(g):
-        return lambda col: [wide[g, (6 - row) * 7 + 6 - col] for row in range(7)]
-
+        return lambda col: [wide[g, (6 - row) * 7 + 6 - col].astype(BF) for row in range(7)]
+
+    for t in range(1, bits):
+        started.append(op_copy(lon, peers[t]))
+        started[-1].start()
     side_weights(k_ref, False, w1)
     prepare(
         owner, index, weight, obs_t, meta, wt, p_mat, pt_mat, obs_slot, height, breadth
@@ -453,6 +456,7 @@
         return carry
 
     lax.fori_loop(0, channels // 16, add_edge, 0, unroll=2)
+    pass_on(1)
 
     side_weights(k_ref, True, w2)
     a, c3 = 0.7978845608028654, 0.044715
@@ -473,8 +477,8 @@
         ana[:, two] = (here + pre * gate).astype(BF)
         return carry
 
-    lax.fori_loop(0, height // 2, ahead, 0, unroll=2)
-    pass_on(1)
+    lax.fori_loop(0, height // 4, ahead, 0, unroll=2)
+    lax.fori_loop(height // 4, height // 2, ahead, 0, unroll=2)
     total = nt(wt[...], ana[...])
     prof[...] = nn(p_mat[...], total.astype(BF)).astype(BF)
 
@@ -603,7 +607,7 @@
             vm((height, channels, breadth), BF),
             vm((height, channels, breadth), BF),
             vm((height, channels, breadth), F32),
-            vm((channels // 16, 49, 16, breadth), BF),
+            vm((channels // 16, 49, 16, breadth), F32),
             vm((21, 8, channels), F32),
             vm((21, 8, channels), F32),
             vm((3, rows, 8, channels), F32),

time: 44.8 us -> 40.9 us (0.913); the launches traced: 44.6 us -> 40.1 us
  Pallas kernels: 41.1 us -> 36.6 us
    pallas_call x1, Pallas kernels: 41.1 us -> 36.6 us  [body(): pl.pallas_call(lambda *refs: kernel(lats, n, *refs), out_shape=(jax.Shape...]
where the time goes in v4:
time: 40.9 us; the launch traced here: 40.1 us
  Pallas kernels  36.6 us (89%)
  local copies, waits for them, and re-layouts  2.85 us (7%)
  between operations  0.65 us (2%)
    pallas_call x1, Pallas kernels, body(): pl.pallas_call(lambda *refs: kernel(lats, n, *refs), out_shape=(jax.Shape...  36.6 us
    unnamed x4, local copies, waits for them, and re-layouts  2.85 us

profile of v4, /device:TPU:1, one launch (start us, length us, event | category | flops | bytes accessed | tf_op | source)
XLA Modules:
  0.0 40.1 jit_solution(17700943991989521117)
XLA Ops:
  0.6 36.6 %shard_map.113 = (bf16[192,16,128]{2,1,0:T(8,128)(2,1)}, bf16[137,512]{1,0:T(8,128)(2,1)}) custom-call(bf16[192,16,128]{2,1,0:T(8,128)(2,1)} %refs_0_.1, bf16[1,192,512]{2,1,0:T(8,128)(2,1)} %refs_1_.1, bf16[1,137,512]{2,1,0:T(8,128)(2,1)} %bitcast.7, bf16[1,137]{1,0:T(2,128)(2,1)} %refs_3_.1, s32[1,512]{1,0:T(1,128)} %bitcast.13, s32[4,512]{1,0:T(4,128)} %bitcast.11, ...), custom_call_target="tpu_custom_call" | custom-call | tf_op jit(solution)/shard_map/pallas_call | solution.py:597
  37.3 0.0 copy-start
  37.3 2.2 %copy.14 = bf16[192,16,128]{2,1,0:T(8,128)(2,1)} copy(bf16[192,16,128]{2,1,0:T(8,128)(2,1)} %get-tuple-element.8) | data formatting | bytes 1572864
  39.5 0.0 copy-done
  39.5 0.7 %copy.15 = bf16[512,137]{0,1:T(8,128)(2,1)} copy(bf16[512,137]{0,1:T(8,128)(2,1)S(1)} %bitcast.9) | data formatting | bytes 280576
Async XLA Ops:
  37.3 2.2 %copy-start = (bf16[137,512]{1,0:T(8,128)(2,1)S(1)}, bf16[137,512]{1,0:T(8,128)(2,1)}, u32[]{:S(2)}) copy-start(bf16[137,512]{1,0:T(8,128)(2,1)} %get-tuple-element.5) | copy-start | bytes 420868

commit v5 on v4

--- a/solution.py
+++ b/solution.py
@@ -545,7 +545,7 @@
         conv_edge(lat_in.at[1], part, flipped(g), pl.multiple_of(g * 16, 16))
         return carry
 
-    lax.fori_loop(0, channels // 16, edge_back, 0, unroll=2)
+    lax.fori_loop(0, channels // 16, edge_back, 0, unroll=4)
 
     def add_side(q, carry):
         r = q * 2
@@ -558,7 +558,7 @@
             )
         return carry
 
-    lax.fori_loop(0, height // 2, add_side, 0, unroll=2)
+    lax.fori_loop(0, height // 2, add_side, 0, unroll=4)
     out_ref[...] = cells[...].astype(BF).reshape(out_ref.shape)
 
 

time: 40.9 us -> 40.3 us (0.985)
  Pallas kernels: 36.6 us -> 36.1 us
    pallas_call x1, Pallas kernels: 36.6 us -> 36.1 us  [body(): pl.pallas_call(lambda *refs: kernel(lats, n, *refs), out_shape=(jax.Shape...]
where the time goes in v5:
time: 40.3 us; the launch traced here: 39.6 us
  Pallas kernels  36.1 us (90%)
  local copies, waits for them, and re-layouts  2.85 us (7%)
  between operations  0.65 us (2%)
    pallas_call x1, Pallas kernels, body(): pl.pallas_call(lambda *refs: kernel(lats, n, *refs), out_shape=(jax.Shape...  36.1 us
    unnamed x4, local copies, waits for them, and re-layouts  2.85 us

profile of v5, /device:TPU:1, one launch (start us, length us, event | category | flops | bytes accessed | tf_op | source)
XLA Modules:
  0.0 39.6 jit_solution(4011971883476814721)
XLA Ops:
  0.6 36.1 %shard_map.113 = (bf16[192,16,128]{2,1,0:T(8,128)(2,1)}, bf16[137,512]{1,0:T(8,128)(2,1)}) custom-call(bf16[192,16,128]{2,1,0:T(8,128)(2,1)} %refs_0_.1, bf16[1,192,512]{2,1,0:T(8,128)(2,1)} %refs_1_.1, bf16[1,137,512]{2,1,0:T(8,128)(2,1)} %bitcast.7, bf16[1,137]{1,0:T(2,128)(2,1)} %refs_3_.1, s32[1,512]{1,0:T(1,128)} %bitcast.13, s32[4,512]{1,0:T(4,128)} %bitcast.11, ...), custom_call_target="tpu_custom_call" | custom-call | tf_op jit(solution)/shard_map/pallas_call | solution.py:597
  36.7 0.0 copy-start
  36.7 2.2 %copy.14 = bf16[192,16,128]{2,1,0:T(8,128)(2,1)} copy(bf16[192,16,128]{2,1,0:T(8,128)(2,1)} %get-tuple-element.8) | data formatting | bytes 1572864
  38.9 0.0 copy-done
  38.9 0.7 %copy.15 = bf16[512,137]{0,1:T(8,128)(2,1)} copy(bf16[512,137]{0,1:T(8,128)(2,1)S(1)} %bitcast.9) | data formatting | bytes 280576
Async XLA Ops:
  36.7 2.2 %copy-start = (bf16[137,512]{1,0:T(8,128)(2,1)S(1)}, bf16[137,512]{1,0:T(8,128)(2,1)}, u32[]{:S(2)}) copy-start(bf16[137,512]{1,0:T(8,128)(2,1)} %get-tuple-element.5) | copy-start | bytes 420868
